TPU v7x, 512 devices: a whole 4x4x16 slice. The times are simulated.
512 devices in a mesh: seq: 64 (over y, z), fsdp: 8 (over x, core).
Axes of the slice: x: 4, y: 4, z: 16, core: 2. Of those that a mesh axis runs over, the one named last changes fastest.
Arguments:
- probe_tensor: bfloat16 [8192, 8, 2048], P('seq', 'fsdp'), may hold values from -10 to 10
- matcher_tensor: bfloat16 [8192, 8, 2048], P('seq', 'fsdp'), may hold values from -10 to 10
- payload_tensor: bfloat16 [8192, 8, 2048], P('seq', 'fsdp'), may hold values from -6 to 6
- adjoint_attended: bfloat16 [8192, 8, 2048], P('seq', 'fsdp'), may hold values from -6 to 6
- logit_scale: float32 [16], replicated, may hold values from 0.5 to 2
- anchor_tiles: int32 [16, 2], replicated, may hold values from 0 to 127, as said below
- sampled_tiles: int32 [16, 128, 3], replicated, may hold values from 0 to 127, as said below
Outputs:
- query_gradients: bfloat16 [8192, 8, 2048], P('seq', 'fsdp')
- grad_key: bfloat16 [8192, 8, 2048], P('seq', 'fsdp')
- grad_value: bfloat16 [8192, 8, 2048], P('seq', 'fsdp')
- adjoint_scales: float32 [16], replicated
Inputs may be any that keep to these rules, and one draw needn't show every extreme that they name: `anchor_tiles`: each head lists 2 different blocks. `sampled_tiles`: each row lists 3 different blocks, none within one block of the row's own block and none among the head's global blocks.
All inputs are finite; a program needn't handle non-finite values.
Results may differ from a plain program's by a relative error of at most 0.0083.
Values may be sent and summed in bfloat16 or wider, within the bound.
No kernel may reach another device: no remote copies, remote signals or barrier semaphores. Data moves between devices by JAX's collectives and lax.ppermute only.
A program may use at most 64 MiB of HBM per device.

v0:
```python
import math
import jax
import jax.numpy as jnp
from jax import lax
from jax.sharding import PartitionSpec as P

TILE_SPAN = 64
masked_minimum = -1e30


def group_of():
    for size in (8, 4, 2):
        return size
    return 1


def block_lists(anchor_tiles, sampled_tiles, nblocks):
    channel_roster = anchor_tiles.shape[0]
    block_ids = jnp.arange(nblocks, dtype=jnp.int32)
    offsets = jnp.array([-1, 0, 1], dtype=jnp.int32)
    window = jnp.broadcast_to(
        (block_ids[:, None] + offsets[None, :])[None], (channel_roster, nblocks, 3)
    )
    window_ok = (window >= 0) & (window < nblocks)
    glob_slots = jnp.broadcast_to(
        anchor_tiles[:, None, :], (channel_roster, nblocks, anchor_tiles.shape[1])
    )
    glob_ok = jnp.abs(glob_slots - block_ids[None, :, None]) > 1
    rand_ok = jnp.ones(sampled_tiles.shape, dtype=bool)
    position_pointer = jnp.concatenate([window, glob_slots, sampled_tiles], axis=2)
    position_pointer = jnp.clip(position_pointer, 0, nblocks - 1)
    position_usable = jnp.concatenate([window_ok, glob_ok, rand_ok], axis=2)
    return (position_pointer, position_usable)


def share_units(device_portion, tok_local, seq_parts, copies, tile_index, tile_span):
    piece = tok_local // copies
    per_piece = piece // tile_index
    units = jnp.arange(seq_parts * per_piece, dtype=jnp.int32)
    position = (
        units // per_piece * tok_local + device_portion * piece + units % per_piece * tile_index
    )
    return position // tile_span


def attend_sample(
    probe_vector,
    matcher_tiles,
    payload_tiles,
    adjoint_signal,
    channel_scale,
    position_pointer,
    position_usable,
    tile_index,
    tile_span,
):
    q_len, channel_width = probe_vector.shape
    k_len = matcher_tiles.shape[0]
    q_units = q_len // tile_index
    k_blocks = k_len // tile_span
    group_size = group_of()
    group_count = q_units // group_size
    reciprocal_sqrt_width = 1.0 / math.sqrt(channel_width)
    key_blocks = matcher_tiles.reshape(k_blocks, tile_span, channel_width)
    value_blocks = payload_tiles.reshape(k_blocks, tile_span, channel_width)
    q_groups = probe_vector.reshape(group_count, group_size, tile_index, channel_width)
    g_groups = adjoint_signal.reshape(group_count, group_size, tile_index, channel_width)
    i_groups = position_pointer.reshape(group_count, group_size, -1)
    v_groups = position_usable.reshape(group_count, group_size, -1)

    def step(carried, inputs):
        key_acc, value_acc, temp_acc = carried
        q_blk, g_blk, idx_blk, ok_blk = inputs
        k_sel = key_blocks[idx_blk]
        v_sel = value_blocks[idx_blk]
        logit_matrix = (
            jnp.einsum("gbd,gsjd->gbsj", q_blk, k_sel, preferred_element_type=jnp.float32)
            * reciprocal_sqrt_width
        )
        position_filter = ok_blk[:, None, :, None]
        rescaled_logits = jnp.where(position_filter, channel_scale * logit_matrix, masked_minimum)
        row_max = jnp.max(rescaled_logits, axis=(2, 3), keepdims=True)
        expo_terms = jnp.where(position_filter, jnp.exp(rescaled_logits - row_max), 0.0)
        row_total = jnp.sum(expo_terms, axis=(2, 3), keepdims=True)
        attn_prob = expo_terms / row_total
        prob_low = attn_prob.astype(jnp.bfloat16)
        d_prob = jnp.einsum("gbd,gsjd->gbsj", g_blk, v_sel, preferred_element_type=jnp.float32)
        row_delta = jnp.sum(attn_prob * d_prob, axis=(2, 3), keepdims=True)
        adjoint_weights = attn_prob * (d_prob - row_delta)
        temp_acc = temp_acc + jnp.sum(adjoint_weights * logit_matrix)
        adjoint_logits = (adjoint_weights * (channel_scale * reciprocal_sqrt_width)).astype(
            jnp.bfloat16
        )
        adjoint_probe = jnp.einsum(
            "gbsj,gsjd->gbd", adjoint_logits, k_sel, preferred_element_type=jnp.float32
        )
        d_keys = jnp.einsum(
            "gbsj,gbd->gsjd", adjoint_logits, q_blk, preferred_element_type=jnp.float32
        )
        d_values = jnp.einsum("gbsj,gbd->gsjd", prob_low, g_blk, preferred_element_type=jnp.float32)
        key_acc = key_acc.at[idx_blk].add(d_keys)
        value_acc = value_acc.at[idx_blk].add(d_values)
        return ((key_acc, value_acc, temp_acc), adjoint_probe.astype(jnp.bfloat16))

    start = (
        jnp.zeros((k_blocks, tile_span, channel_width), jnp.float32),
        jnp.zeros((k_blocks, tile_span, channel_width), jnp.float32),
        jnp.zeros((), jnp.float32),
    )
    (key_acc, value_acc, temp_acc), adjoint_probe = lax.scan(
        step, start, (q_groups, g_groups, i_groups, v_groups)
    )
    return (
        adjoint_probe.reshape(q_len, channel_width),
        key_acc.reshape(k_len, channel_width).astype(jnp.bfloat16),
        value_acc.reshape(k_len, channel_width).astype(jnp.bfloat16),
        temp_acc,
    )


def on_device(
    probe_tensor,
    matcher_tensor,
    payload_tensor,
    adjoint_attended,
    logit_scale,
    anchor_tiles,
    sampled_tiles,
):
    tok_local, seq_count, width = probe_tensor.shape
    channel_roster = logit_scale.shape[0]
    channel_width = width // channel_roster
    seq_parts = lax.axis_size("seq")
    item_total = seq_count * channel_roster
    copies = max(1, seq_parts // item_total)
    per_device = max(1, item_total // seq_parts)
    piece = tok_local // copies
    tile_index = min(TILE_SPAN, piece)

    def to_samples(array):
        return jnp.repeat(array.reshape(tok_local, item_total, channel_width), copies, axis=1)

    def to_shares(array):
        split = array.reshape(copies, piece, item_total, channel_width).transpose(1, 2, 0, 3)
        return split.reshape(piece, item_total * copies, channel_width)

    query_send = to_shares(probe_tensor)
    grad_send = to_shares(adjoint_attended)
    query_item = lax.all_to_all(query_send, "seq", split_axis=1, concat_axis=0, tiled=True)
    key_item = lax.all_to_all(
        to_samples(matcher_tensor), "seq", split_axis=1, concat_axis=0, tiled=True
    )
    value_item = lax.all_to_all(
        to_samples(payload_tensor), "seq", split_axis=1, concat_axis=0, tiled=True
    )
    grad_item = lax.all_to_all(grad_send, "seq", split_axis=1, concat_axis=0, tiled=True)
    length = key_item.shape[0]
    nblocks = length // TILE_SPAN
    my_index = lax.axis_index("seq")
    replica = my_index % copies
    position_pointer, position_usable = block_lists(anchor_tiles, sampled_tiles, nblocks)
    first_item = my_index // copies * per_device
    channel_finder = (first_item + jnp.arange(per_device, dtype=jnp.int32)) % channel_roster
    channel_subset = channel_finder[:, None] == jnp.arange(channel_roster, dtype=jnp.int32)[None, :]
    sample_scales = jnp.sum(jnp.where(channel_subset, logit_scale[None, :], 0.0), axis=1)
    item_index = jnp.sum(
        jnp.where(channel_subset[:, :, None, None], position_pointer[None], 0), axis=1
    )
    item_valid = jnp.any(channel_subset[:, :, None, None] & position_usable[None], axis=1)
    tiles_per_device = share_units(replica, tok_local, seq_parts, copies, tile_index, TILE_SPAN)
    item_index = jnp.take(item_index, tiles_per_device, axis=1)
    item_valid = jnp.take(item_valid, tiles_per_device, axis=1)

    def sample_mapped(sample_operands):
        (
            probe_vector,
            matcher_tiles,
            payload_tiles,
            adjoint_signal,
            channel_scale,
            sample_indices,
            sample_valid_mask,
        ) = sample_operands
        return attend_sample(
            probe_vector,
            matcher_tiles,
            payload_tiles,
            adjoint_signal,
            channel_scale,
            sample_indices,
            sample_valid_mask,
            tile_index,
            TILE_SPAN,
        )

    adjoint_probe, adjoint_matcher, adjoint_payload, adjoint_scale = lax.map(
        sample_mapped,
        (
            jnp.moveaxis(query_item, 1, 0),
            jnp.moveaxis(key_item, 1, 0),
            jnp.moveaxis(value_item, 1, 0),
            jnp.moveaxis(grad_item, 1, 0),
            sample_scales,
            item_index,
            item_valid,
        ),
    )
    scale_pieces = jnp.sum(jnp.where(channel_subset, adjoint_scale[:, None], 0.0), axis=0)
    adjoint_scales = lax.psum(scale_pieces, ("seq", "fsdp"))
    query_grad = jnp.moveaxis(adjoint_probe, 0, 1)
    key_send = jnp.moveaxis(adjoint_matcher, 0, 1)
    value_send = jnp.moveaxis(adjoint_payload, 0, 1)
    back_query = lax.all_to_all(query_grad, "seq", split_axis=0, concat_axis=1, tiled=True)
    returned_key = lax.all_to_all(key_send, "seq", split_axis=0, concat_axis=1, tiled=True)
    returned_value = lax.all_to_all(value_send, "seq", split_axis=0, concat_axis=1, tiled=True)

    def combine_portions(received):
        summed = jnp.sum(
            received.astype(jnp.float32).reshape(tok_local, item_total, copies, channel_width),
            axis=2,
        )
        return summed.astype(jnp.bfloat16).reshape(tok_local, seq_count, width)

    query_gradients = (
        back_query.reshape(piece, item_total, copies, channel_width)
        .transpose(2, 0, 1, 3)
        .reshape(tok_local, seq_count, width)
    )
    return (
        query_gradients,
        combine_portions(returned_key),
        combine_portions(returned_value),
        adjoint_scales,
    )


def solution(mesh):
    placed = (
        P("seq", "fsdp", None),
        P("seq", "fsdp", None),
        P("seq", "fsdp", None),
        P("seq", "fsdp", None),
        P(),
        P(),
        P(),
    )
    return jax.shard_map(
        on_device,
        mesh=mesh,
        in_specs=placed,
        out_specs=(P("seq", "fsdp", None), P("seq", "fsdp", None), P("seq", "fsdp", None), P()),
        check_vma=False,
    )
```

profile of v0, /device:TPU:1, one launch (start us, length us, event | category | flops | bytes accessed | tf_op | source)
XLA Modules:
  0.0 966.9 jit_solution(14185936706878660316)
XLA Ops:
  2.8 19.5 %all-to-all-start = ((bf16[32,64,128]{2,0,1:T(8,128)(2,1)}), bf16[32,64,128]{2,0,1:T(8,128)(2,1)}, u32[]{:S(2)}, u32[]{:S(2)}) async-start(bf16[32,64,128]{2,0,1:T(8,128)(2,1)} %bitcast.24), calls=%async_computation | async-start | bytes 1048576 | tf_op jit(solution)/shard_map/all_to_all | solution.py:149
  23.5 28.3 %all-to-all-done = bf16[32,64,128]{2,0,1:T(8,128)(2,1)} async-done(((bf16[32,64,128]{2,0,1:T(8,128)(2,1)}), bf16[32,64,128]{2,0,1:T(8,128)(2,1)}, u32[]{:S(2)}, u32[]{:S(2)}) %all-to-all-start) | async-done | bytes 524320 | tf_op jit(solution)/shard_map/all_to_all | solution.py:149
  60.8 29.1 %all-to-all-done.2 = bf16[32,64,128]{2,0,1:T(8,128)(2,1)} async-done(((bf16[32,64,128]{2,0,1:T(8,128)(2,1)}), bf16[32,64,128]{2,0,1:T(8,128)(2,1)}, u32[]{:S(2)}, u32[]{:S(2)}) %all-to-all-start.2) | async-done | bytes 524320 | tf_op jit(solution)/shard_map/all_to_all | solution.py:156
  100.9 91.5 %all-to-all-done.1 = bf16[128,64,128]{2,0,1:T(8,128)(2,1)} async-done(((bf16[128,64,128]{2,0,1:T(8,128)(2,1)}), bf16[128,64,128]{2,0,1:T(8,128)(2,1)}, u32[]{:S(2)}, u32[]{:S(2)}) %all-to-all-start.1) | async-done | bytes 2097184 | tf_op jit(solution)/shard_map/all_to_all | solution.py:150
  194.2 14.3 %all-to-all-start.3 = ((bf16[128,64,128]{2,0,1:T(8,128)(2,1)}), bf16[128,64,128]{2,0,1:T(8,128)(2,1)}, u32[]{:S(2)}, u32[]{:S(2)}) async-start(bf16[128,64,128]{2,0,1:T(8,128)(2,1)} %bitcast.37), calls=%async_computation.3 | async-start | bytes 4194304 | tf_op jit(solution)/shard_map/all_to_all | solution.py:153
  212.1 91.3 %all-to-all-done.3 = bf16[128,64,128]{2,0,1:T(8,128)(2,1)} async-done(((bf16[128,64,128]{2,0,1:T(8,128)(2,1)}), bf16[128,64,128]{2,0,1:T(8,128)(2,1)}, u32[]{:S(2)}, u32[]{:S(2)}) %all-to-all-start.3) | async-done | bytes 2097184 | tf_op jit(solution)/shard_map/all_to_all | solution.py:153
  308.3 305.0 %while.32 = (s32[]{:T(128)}, f32[128,64,128]{2,1,0:T(8,128)}, f32[128,64,128]{2,1,0:T(8,128)}, f32[]{:T(128)}, bf16[8,8,32,128]{3,2,1,0:T(8,128)(2,1)}, /*index=...) while((s32[]{:T(128)}, f32[128,64,128]{2,1,0:T(8,128)}, ...), condition=%wide.region_10.11_spmd, body=%wide.region_3.10_spmd.sunk | while | flops 173179328 | bytes 30234488 | solution.py:110
  316.5 10.3 %scatter_fusion.1 = f32[128,64,128]{2,1,0:T(8,128)} fusion(f32[128,64,128]{2,1,0:T(8,128)} %get-tuple-element.349, s32[64]{0:T(128)S(1)} %reshape.476, f32[64,64,128]{2,1,0:T(8,128)} %bitcast.170), kind=kCustom, calls=%fused_computation.5.clone.1 | custom fusion | flops 524288 | bytes 6291712 | tf_op jit(solution)/shard_map/while/body/eval_jaxpr/while/body/eval_jaxpr/scatter-add | solution.py:102
  334.8 9.1 scatter_fusion
  354.6 10.3 %scatter_fusion.1 = f32[128,64,128]{2,1,0:T(8,128)} fusion(f32[128,64,128]{2,1,0:T(8,128)} %get-tuple-element.349, s32[64]{0:T(128)S(1)} %reshape.476, f32[64,64,128]{2,1,0:T(8,128)} %bitcast.170), kind=kCustom, calls=%fused_computation.5.clone.1 | custom fusion | flops 524288 | bytes 6291712 | tf_op jit(solution)/shard_map/while/body/eval_jaxpr/while/body/eval_jaxpr/scatter-add | solution.py:102
  392.7 10.4 %scatter_fusion.1 = f32[128,64,128]{2,1,0:T(8,128)} fusion(f32[128,64,128]{2,1,0:T(8,128)} %get-tuple-element.349, s32[64]{0:T(128)S(1)} %reshape.476, f32[64,64,128]{2,1,0:T(8,128)} %bitcast.170), kind=kCustom, calls=%fused_computation.5.clone.1 | custom fusion | flops 524288 | bytes 6291712 | tf_op jit(solution)/shard_map/while/body/eval_jaxpr/while/body/eval_jaxpr/scatter-add | solution.py:102
  430.9 10.4 %scatter_fusion.1 = f32[128,64,128]{2,1,0:T(8,128)} fusion(f32[128,64,128]{2,1,0:T(8,128)} %get-tuple-element.349, s32[64]{0:T(128)S(1)} %reshape.476, f32[64,64,128]{2,1,0:T(8,128)} %bitcast.170), kind=kCustom, calls=%fused_computation.5.clone.1 | custom fusion | flops 524288 | bytes 6291712 | tf_op jit(solution)/shard_map/while/body/eval_jaxpr/while/body/eval_jaxpr/scatter-add | solution.py:102
  449.2 9.1 scatter_fusion
  469.0 10.3 %scatter_fusion.1 = f32[128,64,128]{2,1,0:T(8,128)} fusion(f32[128,64,128]{2,1,0:T(8,128)} %get-tuple-element.349, s32[64]{0:T(128)S(1)} %reshape.476, f32[64,64,128]{2,1,0:T(8,128)} %bitcast.170), kind=kCustom, calls=%fused_computation.5.clone.1 | custom fusion | flops 524288 | bytes 6291712 | tf_op jit(solution)/shard_map/while/body/eval_jaxpr/while/body/eval_jaxpr/scatter-add | solution.py:102
  507.1 10.4 %scatter_fusion.1 = f32[128,64,128]{2,1,0:T(8,128)} fusion(f32[128,64,128]{2,1,0:T(8,128)} %get-tuple-element.349, s32[64]{0:T(128)S(1)} %reshape.476, f32[64,64,128]{2,1,0:T(8,128)} %bitcast.170), kind=kCustom, calls=%fused_computation.5.clone.1 | custom fusion | flops 524288 | bytes 6291712 | tf_op jit(solution)/shard_map/while/body/eval_jaxpr/while/body/eval_jaxpr/scatter-add | solution.py:102
  545.3 10.4 %scatter_fusion.1 = f32[128,64,128]{2,1,0:T(8,128)} fusion(f32[128,64,128]{2,1,0:T(8,128)} %get-tuple-element.349, s32[64]{0:T(128)S(1)} %reshape.476, f32[64,64,128]{2,1,0:T(8,128)} %bitcast.170), kind=kCustom, calls=%fused_computation.5.clone.1 | custom fusion | flops 524288 | bytes 6291712 | tf_op jit(solution)/shard_map/while/body/eval_jaxpr/while/body/eval_jaxpr/scatter-add | solution.py:102
  563.6 9.1 scatter_fusion
  583.4 10.4 %scatter_fusion.1 = f32[128,64,128]{2,1,0:T(8,128)} fusion(f32[128,64,128]{2,1,0:T(8,128)} %get-tuple-element.349, s32[64]{0:T(128)S(1)} %reshape.476, f32[64,64,128]{2,1,0:T(8,128)} %bitcast.170), kind=kCustom, calls=%fused_computation.5.clone.1 | custom fusion | flops 524288 | bytes 6291712 | tf_op jit(solution)/shard_map/while/body/eval_jaxpr/while/body/eval_jaxpr/scatter-add | solution.py:102
  616.9 10.2 %all-to-all-start.4 = ((bf16[64,2,2048]{2,1,0:T(2,128)(2,1)}), bf16[64,2,2048]{2,1,0:T(2,128)(2,1)S(1)}, u32[]{:S(2)}, u32[]{:S(2)}) async-start(bf16[64,2,2048]{2,1,0:T(2,128)(2,1)} %reshape.453), calls=%async_computation.4 | async-start | bytes 1048576 | tf_op jit(solution)/shard_map/all_to_all | solution.py:213
  636.7 20.0 %all-to-all-done.4 = bf16[64,2,2048]{2,1,0:T(2,128)(2,1)S(1)} async-done(((bf16[64,2,2048]{2,1,0:T(2,128)(2,1)}), bf16[64,2,2048]{2,1,0:T(2,128)(2,1)S(1)}, u32[]{:S(2)}, u32[]{:S(2)}) %all-to-all-start.4) | async-done | bytes 524320 | tf_op jit(solution)/shard_map/all_to_all | solution.py:213
  678.7 78.7 %all-to-all-done.5 = bf16[64,2,8192]{2,1,0:T(2,128)(2,1)S(1)} async-done(((bf16[64,2,8192]{2,1,0:T(2,128)(2,1)}), bf16[64,2,8192]{2,1,0:T(2,128)(2,1)S(1)}, u32[]{:S(2)}, u32[]{:S(2)}) %all-to-all-start.5) | async-done | bytes 2097184 | tf_op jit(solution)/shard_map/all_to_all | solution.py:214
  757.4 14.3 %all-to-all-start.6 = ((bf16[64,2,8192]{2,1,0:T(2,128)(2,1)}), bf16[64,2,8192]{2,1,0:T(2,128)(2,1)}, u32[]{:S(2)}, u32[]{:S(2)}) async-start(bf16[64,2,8192]{2,1,0:T(2,128)(2,1)} %reshape.457), calls=%async_computation.6 | async-start | bytes 4194304 | tf_op jit(solution)/shard_map/all_to_all | solution.py:215
  771.7 164.4 %psum.7 = f32[16]{0:T(128)} all-reduce(f32[16]{0:T(128)S(1)} %broadcast_select_fusion), channel_id=1, replica_groups=mesh['seq'=64,'fsdp'=8] {'seq','fsdp'}, use_global_device_ids=true, to_apply=%region_13.14 | all-reduce | flops 16 | bytes 128 | tf_op jit(solution)/shard_map/psum | solution.py:209
  952.2 10.4 %reshape.458 = bf16[8192,1,128]{2,1,0:T(2,128)(2,1)} reshape(bf16[64,2,8192]{2,1,0:T(2,128)(2,1)} %all-to-all-done.6) | data formatting | bytes 4194304
  (204 shorter events, 277.8 us)
Async XLA Ops:
  0.6 21.7 %copy-start.2 = (bf16[128,1,2048]{2,0,1:T(8,128)(2,1)S(1)}, bf16[128,1,2048]{2,0,1:T(8,128)(2,1)}, u32[]{:S(2)}) copy-start(bf16[128,1,2048]{2,0,1:T(8,128)(2,1)} %param.13) | copy-start | bytes 1572868
  2.8 48.9 %all-to-all-start = ((bf16[32,64,128]{2,0,1:T(8,128)(2,1)}), bf16[32,64,128]{2,0,1:T(8,128)(2,1)}, u32[]{:S(2)}, u32[]{:S(2)}) async-start(bf16[32,64,128]{2,0,1:T(8,128)(2,1)} %bitcast.24), calls=%async_computation | async-start | bytes 1048576 | tf_op jit(solution)/shard_map/all_to_all | solution.py:149
  22.4 38.2 %copy-start.3 = (bf16[128,1,2048]{2,0,1:T(8,128)(2,1)S(1)}, bf16[128,1,2048]{2,0,1:T(8,128)(2,1)}, u32[]{:S(2)}) copy-start(bf16[128,1,2048]{2,0,1:T(8,128)(2,1)} %param.11) | copy-start | bytes 1572868
  51.7 38.1 %all-to-all-start.2 = ((bf16[32,64,128]{2,0,1:T(8,128)(2,1)}), bf16[32,64,128]{2,0,1:T(8,128)(2,1)}, u32[]{:S(2)}, u32[]{:S(2)}) async-start(bf16[32,64,128]{2,0,1:T(8,128)(2,1)} %bitcast.33), calls=%async_computation.2 | async-start | bytes 1048576 | tf_op jit(solution)/shard_map/all_to_all | solution.py:156
  91.7 8.9 copy-start.4
  91.7 100.6 %all-to-all-start.1 = ((bf16[128,64,128]{2,0,1:T(8,128)(2,1)}), bf16[128,64,128]{2,0,1:T(8,128)(2,1)}, u32[]{:S(2)}, u32[]{:S(2)}) async-start(bf16[128,64,128]{2,0,1:T(8,128)(2,1)} %bitcast.28), calls=%async_computation.1 | async-start | bytes 4194304 | tf_op jit(solution)/shard_map/all_to_all | solution.py:150
  194.2 14.4 %copy-start.7 = (s32[3]{0:T(128)S(1)}, s32[3]{0:T(128)}, u32[]{:S(2)}) copy-start(s32[3]{0:T(128)} %constant.217.clone) | copy-start | bytes 40
  194.2 14.5 %copy-start.6 = (s32[16,2]{0,1:T(2,128)S(1)}, s32[16,2]{0,1:T(2,128)}, u32[]{:S(2)}) copy-start(s32[16,2]{0,1:T(2,128)} %param.15) | copy-start | bytes 388
  194.2 14.6 %copy-start.5 = (s32[16,128,3]{1,0,2:T(8,128)S(1)}, s32[16,128,3]{1,0,2:T(8,128)}, u32[]{:S(2)}) copy-start(s32[16,128,3]{1,0,2:T(8,128)} %param.16) | copy-start | bytes 73732
  194.2 16.5 %copy-start.8 = (f32[16]{0:T(128)S(1)}, f32[16]{0:T(128)}, u32[]{:S(2)}) copy-start(f32[16]{0:T(128)} %param.14) | copy-start | bytes 196
  194.2 109.2 %all-to-all-start.3 = ((bf16[128,64,128]{2,0,1:T(8,128)(2,1)}), bf16[128,64,128]{2,0,1:T(8,128)(2,1)}, u32[]{:S(2)}, u32[]{:S(2)}) async-start(bf16[128,64,128]{2,0,1:T(8,128)(2,1)} %bitcast.37), calls=%async_computation.3 | async-start | bytes 4194304 | tf_op jit(solution)/shard_map/all_to_all | solution.py:153
  332.6 0.8 copy-start
  370.8 0.8 copy-start
  408.9 0.8 copy-start
  447.0 0.8 copy-start
  485.2 0.8 copy-start
  523.3 0.8 copy-start
  561.4 0.8 copy-start
  599.6 0.8 copy-start
  616.9 39.7 %all-to-all-start.4 = ((bf16[64,2,2048]{2,1,0:T(2,128)(2,1)}), bf16[64,2,2048]{2,1,0:T(2,128)(2,1)S(1)}, u32[]{:S(2)}, u32[]{:S(2)}) async-start(bf16[64,2,2048]{2,1,0:T(2,128)(2,1)} %reshape.453), calls=%async_computation.4 | async-start | bytes 1048576 | tf_op jit(solution)/shard_map/all_to_all | solution.py:213
  656.6 0.8 copy-start.1
  657.4 100.0 %all-to-all-start.5 = ((bf16[64,2,8192]{2,1,0:T(2,128)(2,1)}), bf16[64,2,8192]{2,1,0:T(2,128)(2,1)S(1)}, u32[]{:S(2)}, u32[]{:S(2)}) async-start(bf16[64,2,8192]{2,1,0:T(2,128)(2,1)} %reshape.455), calls=%async_computation.5 | async-start | bytes 4194304 | tf_op jit(solution)/shard_map/all_to_all | solution.py:214
  757.4 194.8 %all-to-all-start.6 = ((bf16[64,2,8192]{2,1,0:T(2,128)(2,1)}), bf16[64,2,8192]{2,1,0:T(2,128)(2,1)}, u32[]{:S(2)}, u32[]{:S(2)}) async-start(bf16[64,2,8192]{2,1,0:T(2,128)(2,1)} %reshape.457), calls=%async_computation.6 | async-start | bytes 4194304 | tf_op jit(solution)/shard_map/all_to_all | solution.py:215
where the time goes:
time: 975 us; the launch traced here: 967 us
  waiting for transfers between devices  339 us (35%)
  other arithmetic  189 us (19%)
  blocking collectives  164 us (17%)
  local copies, waits for them, and re-layouts  98.4 us (10%)
  starting transfers between devices  84.8 us (9%)
  matrix products  84.5 us (9%)
    psum x1, blocking collectives, on_device(): adjoint_scales = lax.psum(scale_pieces, ('seq', 'fsdp'))  164 us
    all_to_all x1, waiting for transfers between devices, on_device(): lax.all_to_all(to_samples(matcher_tensor), 'seq', split_axis=1, concat_ax...  91.5 us
    all_to_all x1, waiting for transfers between devices, on_device(): lax.all_to_all(to_samples(payload_tensor), 'seq', split_axis=1, concat_ax...  91.3 us
    scatter-add x8, other arithmetic, step(): value_acc = value_acc.at[idx_blk].add(d_values)  82.8 us
    all_to_all x1, waiting for transfers between devices, on_device(): lax.all_to_all(key_send, 'seq', split_axis=0, concat_axis=1, tiled=True)  78.7 us
    scatter-add x8, other arithmetic, step(): key_acc = key_acc.at[idx_blk].add(d_keys)  72.5 us
    unnamed x31, local copies, waits for them, and re-layouts  39 us
    all_to_all x1, waiting for transfers between devices, on_device(): lax.all_to_all(grad_send, 'seq', split_axis=1, concat_axis=0, tiled=True)  29.1 us
  transfers between devices with their start and end apart: 7, of which 6 were waited for; matrix products, arithmetic and copies ran while one was open for 4% of the time, Pallas kernels for 0%

commit v1 on v0

--- a/solution.py
+++ b/solution.py
@@ -206,7 +206,7 @@
         ),
     )
     scale_pieces = jnp.sum(jnp.where(channel_subset, adjoint_scale[:, None], 0.0), axis=0)
-    adjoint_scales = lax.psum(scale_pieces, ("seq", "fsdp"))
+    adjoint_scales = lax.psum(lax.psum(scale_pieces, "seq"), "fsdp")
     query_grad = jnp.moveaxis(adjoint_probe, 0, 1)
     key_send = jnp.moveaxis(adjoint_matcher, 0, 1)
     value_send = jnp.moveaxis(adjoint_payload, 0, 1)

time: 975 us -> 1050 us (1.077)
  blocking collectives: 164 us -> 238 us
    psum x1 -> x2, blocking collectives: 164 us -> 238 us  [on_device(): adjoint_scales = lax.psum(lax.psum(scale_pieces, 'seq'), 'fsdp')]
where the time goes in v1:
time: 1050 us; the launch traced here: 1040 us
  waiting for transfers between devices  339 us (32%)
  blocking collectives  238 us (23%)
  other arithmetic  189 us (18%)
  local copies, waits for them, and re-layouts  98.4 us (9%)
  starting transfers between devices  84.8 us (8%)
  matrix products  84.5 us (8%)
    psum x2, blocking collectives, on_device(): adjoint_scales = lax.psum(lax.psum(scale_pieces, 'seq'), 'fsdp')  238 us
    all_to_all x1, waiting for transfers between devices, on_device(): lax.all_to_all(to_samples(matcher_tensor), 'seq', split_axis=1, concat_ax...  91.5 us
    all_to_all x1, waiting for transfers between devices, on_device(): lax.all_to_all(to_samples(payload_tensor), 'seq', split_axis=1, concat_ax...  91.3 us
    scatter-add x8, other arithmetic, step(): value_acc = value_acc.at[idx_blk].add(d_values)  82.8 us
    all_to_all x1, waiting for transfers between devices, on_device(): lax.all_to_all(key_send, 'seq', split_axis=0, concat_axis=1, tiled=True)  78.7 us
    scatter-add x8, other arithmetic, step(): key_acc = key_acc.at[idx_blk].add(d_keys)  72.5 us
    unnamed x31, local copies, waits for them, and re-layouts  39 us
    all_to_all x1, waiting for transfers between devices, on_device(): lax.all_to_all(grad_send, 'seq', split_axis=1, concat_axis=0, tiled=True)  29.1 us
  transfers between devices with their start and end apart: 7, of which 6 were waited for; matrix products, arithmetic and copies ran while one was open for 4% of the time, Pallas kernels for 0%

profile of v1, /device:TPU:1, one launch (start us, length us, event | category | flops | bytes accessed | tf_op | source)
XLA Modules:
  0.0 1040.2 jit_solution(6756276460864452721)
XLA Ops:
  2.8 19.5 %all-to-all-start = ((bf16[32,64,128]{2,0,1:T(8,128)(2,1)}), bf16[32,64,128]{2,0,1:T(8,128)(2,1)}, u32[]{:S(2)}, u32[]{:S(2)}) async-start(bf16[32,64,128]{2,0,1:T(8,128)(2,1)} %bitcast.24), calls=%async_computation | async-start | bytes 1048576 | tf_op jit(solution)/shard_map/all_to_all | solution.py:149
  23.5 28.3 %all-to-all-done = bf16[32,64,128]{2,0,1:T(8,128)(2,1)} async-done(((bf16[32,64,128]{2,0,1:T(8,128)(2,1)}), bf16[32,64,128]{2,0,1:T(8,128)(2,1)}, u32[]{:S(2)}, u32[]{:S(2)}) %all-to-all-start) | async-done | bytes 524320 | tf_op jit(solution)/shard_map/all_to_all | solution.py:149
  60.8 29.1 %all-to-all-done.2 = bf16[32,64,128]{2,0,1:T(8,128)(2,1)} async-done(((bf16[32,64,128]{2,0,1:T(8,128)(2,1)}), bf16[32,64,128]{2,0,1:T(8,128)(2,1)}, u32[]{:S(2)}, u32[]{:S(2)}) %all-to-all-start.2) | async-done | bytes 524320 | tf_op jit(solution)/shard_map/all_to_all | solution.py:156
  100.9 91.5 %all-to-all-done.1 = bf16[128,64,128]{2,0,1:T(8,128)(2,1)} async-done(((bf16[128,64,128]{2,0,1:T(8,128)(2,1)}), bf16[128,64,128]{2,0,1:T(8,128)(2,1)}, u32[]{:S(2)}, u32[]{:S(2)}) %all-to-all-start.1) | async-done | bytes 2097184 | tf_op jit(solution)/shard_map/all_to_all | solution.py:150
  194.2 14.3 %all-to-all-start.3 = ((bf16[128,64,128]{2,0,1:T(8,128)(2,1)}), bf16[128,64,128]{2,0,1:T(8,128)(2,1)}, u32[]{:S(2)}, u32[]{:S(2)}) async-start(bf16[128,64,128]{2,0,1:T(8,128)(2,1)} %bitcast.37), calls=%async_computation.3 | async-start | bytes 4194304 | tf_op jit(solution)/shard_map/all_to_all | solution.py:153
  212.1 91.3 %all-to-all-done.3 = bf16[128,64,128]{2,0,1:T(8,128)(2,1)} async-done(((bf16[128,64,128]{2,0,1:T(8,128)(2,1)}), bf16[128,64,128]{2,0,1:T(8,128)(2,1)}, u32[]{:S(2)}, u32[]{:S(2)}) %all-to-all-start.3) | async-done | bytes 2097184 | tf_op jit(solution)/shard_map/all_to_all | solution.py:153
  308.3 305.0 %while.32 = (s32[]{:T(128)}, f32[128,64,128]{2,1,0:T(8,128)}, f32[128,64,128]{2,1,0:T(8,128)}, f32[]{:T(128)}, bf16[8,8,32,128]{3,2,1,0:T(8,128)(2,1)}, /*index=...) while((s32[]{:T(128)}, f32[128,64,128]{2,1,0:T(8,128)}, ...), condition=%wide.region_10.11_spmd, body=%wide.region_3.10_spmd.sunk | while | flops 173179328 | bytes 30234488 | solution.py:110
  316.5 10.3 scatter_fusion.1
  334.8 9.1 scatter_fusion
  354.6 10.3 scatter_fusion.1
  392.7 10.4 scatter_fusion.1
  430.9 10.4 scatter_fusion.1
  449.2 9.1 scatter_fusion
  469.0 10.3 scatter_fusion.1
  507.1 10.4 scatter_fusion.1
  545.3 10.4 scatter_fusion.1
  583.4 10.4 scatter_fusion.1
  616.9 10.2 all-to-all-start.4
  636.7 20.0 %all-to-all-done.4 = bf16[64,2,2048]{2,1,0:T(2,128)(2,1)S(1)} async-done(((bf16[64,2,2048]{2,1,0:T(2,128)(2,1)}), bf16[64,2,2048]{2,1,0:T(2,128)(2,1)S(1)}, u32[]{:S(2)}, u32[]{:S(2)}) %all-to-all-start.4) | async-done | bytes 524320 | tf_op jit(solution)/shard_map/all_to_all | solution.py:213
  678.7 78.7 %all-to-all-done.5 = bf16[64,2,8192]{2,1,0:T(2,128)(2,1)S(1)} async-done(((bf16[64,2,8192]{2,1,0:T(2,128)(2,1)}), bf16[64,2,8192]{2,1,0:T(2,128)(2,1)S(1)}, u32[]{:S(2)}, u32[]{:S(2)}) %all-to-all-start.5) | async-done | bytes 2097184 | tf_op jit(solution)/shard_map/all_to_all | solution.py:214
  757.4 14.3 %all-to-all-start.6 = ((bf16[64,2,8192]{2,1,0:T(2,128)(2,1)}), bf16[64,2,8192]{2,1,0:T(2,128)(2,1)}, u32[]{:S(2)}, u32[]{:S(2)}) async-start(bf16[64,2,8192]{2,1,0:T(2,128)(2,1)} %reshape.457), calls=%async_computation.6 | async-start | bytes 4194304 | tf_op jit(solution)/shard_map/all_to_all | solution.py:215
  771.7 197.0 %psum.14 = f32[16]{0:T(128)S(1)} all-reduce(f32[16]{0:T(128)S(1)} %broadcast_select_fusion), channel_id=1, replica_groups=mesh['seq'=64,'fsdp'=8] {'seq'}, use_global_device_ids=true, to_apply=%region_13.14 | all-reduce | flops 16 | bytes 128 | tf_op jit(solution)/shard_map/psum | solution.py:209
  968.7 40.7 %psum.15 = f32[16]{0:T(128)} all-reduce(f32[16]{0:T(128)S(1)} %psum.14), channel_id=1, replica_groups=mesh['seq'=64,'fsdp'=8] {'fsdp'}, use_global_device_ids=true, to_apply=%region_14.15 | all-reduce | flops 16 | bytes 128 | tf_op jit(solution)/shard_map/psum | solution.py:209
  1025.5 10.4 %reshape.458 = bf16[8192,1,128]{2,1,0:T(2,128)(2,1)} reshape(bf16[64,2,8192]{2,1,0:T(2,128)(2,1)} %all-to-all-done.6) | data formatting | bytes 4194304
  (205 shorter events, 286.8 us)
Async XLA Ops:
  0.6 21.7 %copy-start.2 = (bf16[128,1,2048]{2,0,1:T(8,128)(2,1)S(1)}, bf16[128,1,2048]{2,0,1:T(8,128)(2,1)}, u32[]{:S(2)}) copy-start(bf16[128,1,2048]{2,0,1:T(8,128)(2,1)} %param.13) | copy-start | bytes 1572868
  2.8 48.9 %all-to-all-start = ((bf16[32,64,128]{2,0,1:T(8,128)(2,1)}), bf16[32,64,128]{2,0,1:T(8,128)(2,1)}, u32[]{:S(2)}, u32[]{:S(2)}) async-start(bf16[32,64,128]{2,0,1:T(8,128)(2,1)} %bitcast.24), calls=%async_computation | async-start | bytes 1048576 | tf_op jit(solution)/shard_map/all_to_all | solution.py:149
  22.4 38.2 %copy-start.3 = (bf16[128,1,2048]{2,0,1:T(8,128)(2,1)S(1)}, bf16[128,1,2048]{2,0,1:T(8,128)(2,1)}, u32[]{:S(2)}) copy-start(bf16[128,1,2048]{2,0,1:T(8,128)(2,1)} %param.11) | copy-start | bytes 1572868
  51.7 38.1 %all-to-all-start.2 = ((bf16[32,64,128]{2,0,1:T(8,128)(2,1)}), bf16[32,64,128]{2,0,1:T(8,128)(2,1)}, u32[]{:S(2)}, u32[]{:S(2)}) async-start(bf16[32,64,128]{2,0,1:T(8,128)(2,1)} %bitcast.33), calls=%async_computation.2 | async-start | bytes 1048576 | tf_op jit(solution)/shard_map/all_to_all | solution.py:156
  91.7 8.9 copy-start.4
  91.7 100.6 %all-to-all-start.1 = ((bf16[128,64,128]{2,0,1:T(8,128)(2,1)}), bf16[128,64,128]{2,0,1:T(8,128)(2,1)}, u32[]{:S(2)}, u32[]{:S(2)}) async-start(bf16[128,64,128]{2,0,1:T(8,128)(2,1)} %bitcast.28), calls=%async_computation.1 | async-start | bytes 4194304 | tf_op jit(solution)/shard_map/all_to_all | solution.py:150
  194.2 14.4 %copy-start.7 = (s32[3]{0:T(128)S(1)}, s32[3]{0:T(128)}, u32[]{:S(2)}) copy-start(s32[3]{0:T(128)} %constant.217.clone) | copy-start | bytes 40
  194.2 14.5 %copy-start.6 = (s32[16,2]{0,1:T(2,128)S(1)}, s32[16,2]{0,1:T(2,128)}, u32[]{:S(2)}) copy-start(s32[16,2]{0,1:T(2,128)} %param.15) | copy-start | bytes 388
  194.2 14.6 %copy-start.5 = (s32[16,128,3]{1,0,2:T(8,128)S(1)}, s32[16,128,3]{1,0,2:T(8,128)}, u32[]{:S(2)}) copy-start(s32[16,128,3]{1,0,2:T(8,128)} %param.16) | copy-start | bytes 73732
  194.2 16.5 %copy-start.8 = (f32[16]{0:T(128)S(1)}, f32[16]{0:T(128)}, u32[]{:S(2)}) copy-start(f32[16]{0:T(128)} %param.14) | copy-start | bytes 196
  194.2 109.2 %all-to-all-start.3 = ((bf16[128,64,128]{2,0,1:T(8,128)(2,1)}), bf16[128,64,128]{2,0,1:T(8,128)(2,1)}, u32[]{:S(2)}, u32[]{:S(2)}) async-start(bf16[128,64,128]{2,0,1:T(8,128)(2,1)} %bitcast.37), calls=%async_computation.3 | async-start | bytes 4194304 | tf_op jit(solution)/shard_map/all_to_all | solution.py:153
  332.6 0.8 copy-start
  370.8 0.8 copy-start
  408.9 0.8 copy-start
  447.0 0.8 copy-start
  485.2 0.8 copy-start
  523.3 0.8 copy-start
  561.4 0.8 copy-start
  599.6 0.8 copy-start
  616.9 39.7 %all-to-all-start.4 = ((bf16[64,2,2048]{2,1,0:T(2,128)(2,1)}), bf16[64,2,2048]{2,1,0:T(2,128)(2,1)S(1)}, u32[]{:S(2)}, u32[]{:S(2)}) async-start(bf16[64,2,2048]{2,1,0:T(2,128)(2,1)} %reshape.453), calls=%async_computation.4 | async-start | bytes 1048576 | tf_op jit(solution)/shard_map/all_to_all | solution.py:213
  656.6 0.8 copy-start.1
  657.4 100.0 %all-to-all-start.5 = ((bf16[64,2,8192]{2,1,0:T(2,128)(2,1)}), bf16[64,2,8192]{2,1,0:T(2,128)(2,1)S(1)}, u32[]{:S(2)}, u32[]{:S(2)}) async-start(bf16[64,2,8192]{2,1,0:T(2,128)(2,1)} %reshape.455), calls=%async_computation.5 | async-start | bytes 4194304 | tf_op jit(solution)/shard_map/all_to_all | solution.py:214
  757.4 268.1 %all-to-all-start.6 = ((bf16[64,2,8192]{2,1,0:T(2,128)(2,1)}), bf16[64,2,8192]{2,1,0:T(2,128)(2,1)}, u32[]{:S(2)}, u32[]{:S(2)}) async-start(bf16[64,2,8192]{2,1,0:T(2,128)(2,1)} %reshape.457), calls=%async_computation.6 | async-start | bytes 4194304 | tf_op jit(solution)/shard_map/all_to_all | solution.py:215
